TPU v7x, 32 devices: a whole 2x2x4 slice. The times are simulated.
32 devices in a mesh: row: 16 (over z, x, core), col: 2 (over y).
Axes of the slice: x: 2, y: 2, z: 4, core: 2. Of those that a mesh axis runs over, the one named last changes fastest.
Arguments:
- pair_rep: bfloat16 [256, 256, 128], P('row', 'col'), may hold values from -6 to 6
- chain_len: int32 [4], replicated, may hold values from 1 to 64, as said below
- tri_gain: float32 [128], replicated, may hold values from 0.5 to 2
- tri_in: bfloat16 [128, 640], replicated, may hold values from -0.5 to 0.5
- sum_gain: float32 [128], replicated, may hold values from 0.5 to 2
- tri_out: bfloat16 [128, 128], replicated, may hold values from -0.5 to 0.5
- att_gain: float32 [128], replicated, may hold values from 0.5 to 8
- att_in: bfloat16 [128, 512], replicated, may hold values from -0.5 to 0.5
- att_bias: bfloat16 [128, 4], replicated, may hold values from -2 to 2
- att_out: bfloat16 [128, 128], replicated, may hold values from -4 to 4
Outputs:
- new_pair: bfloat16 [256, 256, 128], P('row', 'col')
Inputs may be any that keep to these rules, and one draw needn't show every extreme that they name: `chain_len`: one chain in every draw has all 64 slots live.
All inputs are finite; a program needn't handle non-finite values.
Results may differ from a plain program's by a relative error of at most 0.039.
The roundings to bfloat16 on the way count: a program that leaves them out, or rounds other values in their place, can miss the bound.
Values may be sent and summed in bfloat16 or wider, within the bound.
No kernel may reach another device: no remote copies, remote signals or barrier semaphores. Data moves between devices by JAX's collectives and lax.ppermute only.
A program may use at most 128 MiB of HBM per device.

v0:
```python
import math
import jax
import jax.numpy as jnp
from jax import lax
from jax.sharding import PartitionSpec as P

CH = 128
H = 4
DH = 32
KCD = 16
SLOT = 64
EPSILON = 1e-05
NEG_SCORE = -1e30


def layer_norm(values, norm_gain):
    values = values.astype(jnp.float32)
    centre = values - jnp.mean(values, axis=-1, keepdims=True)
    spread = jnp.mean(centre * centre, axis=-1, keepdims=True)
    return centre * lax.rsqrt(spread + EPSILON) * norm_gain


def live_tokens(chain_len):
    positions = lax.broadcasted_iota(jnp.int32, (chain_len.shape[0], SLOT), 1)
    return (positions < chain_len[:, None]).astype(jnp.float32).reshape(-1)


def attend_heads(query_pair, kv_all, bias_pair, key_live):

    def attend_row(inputs):
        query_row, kv_row = inputs
        keys_row = kv_row[:, : 2 * DH].reshape(kv_row.shape[0], 2, DH)
        values_row = kv_row[:, 2 * DH :].reshape(kv_row.shape[0], 2, DH)
        scores = (
            jnp.einsum("jhd,khd->hjk", query_row, keys_row, preferred_element_type=jnp.float32)
            / math.sqrt(DH)
            + bias_pair
        )
        scores = jnp.where(key_live[None, None, :], scores, NEG_SCORE)
        row_top = jnp.max(scores, axis=-1, keepdims=True)
        weights = jnp.exp(scores - row_top).astype(jnp.bfloat16)
        totals = jnp.sum(weights, axis=-1, dtype=jnp.float32)
        summed = jnp.einsum("hjk,khd->jhd", weights, values_row, preferred_element_type=jnp.float32)
        return summed / jnp.transpose(totals)[:, :, None]

    return lax.map(attend_row, (query_pair, kv_all))


def body(
    pair_rep, chain_len, tri_gain, tri_in, sum_gain, tri_out, att_gain, att_in, att_bias, att_out
):
    row_count = pair_rep.shape[0]
    col_count = pair_rep.shape[1]
    row_start = lax.axis_index("row") * row_count
    col_start = lax.axis_index("col") * col_count
    live_all = live_tokens(chain_len)
    live_rows = lax.dynamic_slice_in_dim(live_all, row_start, row_count)
    live_cols = lax.dynamic_slice_in_dim(live_all, col_start, col_count)
    tri_norm = layer_norm(pair_rep, tri_gain).astype(jnp.bfloat16)
    out_gate = jax.nn.sigmoid(
        jnp.dot(tri_norm, tri_in[:, 4 * CH :], preferred_element_type=jnp.float32)
    )
    group_proj = jnp.dot(tri_norm[:, :KCD], tri_in[:, : 4 * CH], preferred_element_type=jnp.float32)
    pair_live = live_rows[:, None, None] * live_cols[None, :KCD, None]
    left_edge = (
        jax.nn.sigmoid(group_proj[..., :CH]) * group_proj[..., CH : 2 * CH] * pair_live
    ).astype(jnp.bfloat16)
    right_edge = (
        jax.nn.sigmoid(group_proj[..., 2 * CH : 3 * CH])
        * group_proj[..., 3 * CH : 4 * CH]
        * pair_live
    ).astype(jnp.bfloat16)
    right_all = lax.all_gather(right_edge, "row", axis=0, tiled=True)
    right_cols = lax.all_to_all(right_all, "col", split_axis=0, concat_axis=1, tiled=True)
    left_all = lax.all_gather(left_edge, "col", axis=1, tiled=True)
    tri_sum = jnp.einsum("ikc,jkc->jic", left_all, right_cols, preferred_element_type=jnp.float32)
    sum_norm = layer_norm(tri_sum, sum_gain).astype(jnp.bfloat16)
    update = jnp.dot(sum_norm, tri_out, preferred_element_type=jnp.float32)
    mid_pair = (pair_rep.astype(jnp.float32) + out_gate * jnp.transpose(update, (1, 0, 2))).astype(
        jnp.bfloat16
    )
    head_width = H * DH
    att_norm = layer_norm(mid_pair, att_gain).astype(jnp.bfloat16)
    queries = jnp.dot(att_norm, att_in[:, :head_width], preferred_element_type=jnp.float32).astype(
        jnp.bfloat16
    )
    att_gate = jax.nn.sigmoid(
        jnp.dot(att_norm, att_in[:, 3 * head_width :], preferred_element_type=jnp.float32)
    )
    pair_bias = jnp.einsum(
        "rcd,dh->hrc", att_norm, att_bias, preferred_element_type=jnp.float32
    ).astype(jnp.bfloat16)
    bias_rows = lax.all_gather(pair_bias, "row", axis=1, tiled=True)
    bias_local = lax.all_to_all(bias_rows, "col", split_axis=1, concat_axis=2, tiled=True)
    key_live = live_all > 0.5
    pieces = []
    for pair_index in range(H // 2):
        head_low = 2 * pair_index * DH
        head_high = head_low + 2 * DH
        kv_weight = jnp.concatenate(
            [
                att_in[:, head_width + head_low : head_width + head_high],
                att_in[:, 2 * head_width + head_low : 2 * head_width + head_high],
            ],
            axis=1,
        )
        kv_local = jnp.dot(att_norm, kv_weight, preferred_element_type=jnp.float32).astype(
            jnp.bfloat16
        )
        kv_all = lax.all_gather(kv_local, "col", axis=1, tiled=True)
        query_pair = queries[:, :, head_low:head_high].reshape(row_count, col_count, 2, DH)
        bias_pair = bias_local[2 * pair_index : 2 * pair_index + 2]
        pieces.append(attend_heads(query_pair, kv_all, bias_pair, key_live))
    attended = jnp.concatenate(pieces, axis=2).reshape(row_count, col_count, head_width)
    attended = (attended * att_gate).astype(jnp.bfloat16)
    new_pair = (
        mid_pair.astype(jnp.float32)
        + jnp.dot(attended, att_out, preferred_element_type=jnp.float32)
    ).astype(jnp.bfloat16)
    return new_pair


def solution(mesh):
    placed = (P("row", "col", None), P(), P(), P(), P(), P(), P(), P(), P(), P())
    return jax.shard_map(
        body, mesh=mesh, in_specs=placed, out_specs=P("row", "col", None), check_vma=False
    )
```

profile of v0, /device:TPU:0, one launch (start us, length us, event | category | flops | bytes accessed | tf_op | source)
XLA Modules:
  0.0 187.7 jit_solution(6166348117230079474)
XLA Ops:
  7.5 1.3 copy.31
  11.8 40.7 %all-gather.4.cloned.1.call-done = bf16[256,16,128]{2,1,0:T(8,128)(2,1)} async-done(((bf16[16,16,128]{2,1,0:T(8,128)(2,1)}), bf16[256,16,128]{2,1,0:T(8,128)(2,1)}) %all-gather.4.cloned.1.call-update) | async-done | bytes 1048592 | tf_op jit(solution)/shard_map/all_gather | solution.py:73
  52.5 3.6 %all-to-all-start = ((bf16[256,16,128]{2,1,0:T(8,128)(2,1)}), bf16[256,16,128]{2,1,0:T(8,128)(2,1)S(1)}, u32[]{:S(2)}, u32[]{:S(2)}) async-start(bf16[256,16,128]{2,1,0:T(8,128)(2,1)} %all-gather.4.cloned.1.call-done), calls=%async_computation | async-start | bytes 2097152 | tf_op jit(solution)/shard_map/all_to_all | solution.py:74
  56.1 15.6 %all_gather.16 = bf16[16,32,128]{2,1,0:T(8,128)(2,1)S(1)} all-gather(bf16[16,16,128]{2,1,0:T(8,128)(2,1)S(1)} %get-tuple-element.154), channel_id=1, replica_groups=mesh['row'=16,'col'=2] {'col'}, dimensions={1}, use_global_device_ids=true | all-gather | bytes 196608 | tf_op jit(solution)/shard_map/all_gather | solution.py:75
  72.7 1.5 fusion.45
  74.2 1.5 copy.35
  78.8 1.2 convolution_convert_fusion.2
  81.0 21.5 %all_gather.18 = bf16[4,256,128]{2,0,1:T(4,128)(2,1)} all-gather(bf16[4,16,128]{2,0,1:T(4,128)(2,1)S(1)} %fusion.53), channel_id=1, replica_groups=mesh['row'=16,'col'=2] {'row'}, dimensions={1}, use_global_device_ids=true | all-gather | bytes 278528 | tf_op jit(solution)/shard_map/all_gather | solution.py:93
  102.5 3.4 %all-to-all-start.1 = ((bf16[4,256,128]{2,0,1:T(4,128)(2,1)}), bf16[4,256,128]{2,0,1:T(4,128)(2,1)S(1)}, u32[]{:S(2)}, u32[]{:S(2)}) async-start(bf16[4,256,128]{2,0,1:T(4,128)(2,1)} %all_gather.18), calls=%async_computation.1 | async-start | bytes 524288 | tf_op jit(solution)/shard_map/all_to_all | solution.py:94
  106.0 1.2 convolution_convert_fusion.1
  107.6 4.2 %all-to-all-done.1 = bf16[4,256,128]{2,0,1:T(4,128)(2,1)S(1)} async-done(((bf16[4,256,128]{2,0,1:T(4,128)(2,1)}), bf16[4,256,128]{2,0,1:T(4,128)(2,1)S(1)}, u32[]{:S(2)}, u32[]{:S(2)}) %all-to-all-start.1) | async-done | bytes 262176 | tf_op jit(solution)/shard_map/all_to_all | solution.py:94
  112.6 33.0 %while.22 = (s32[]{:T(128)}, f32[16,128,2,32]{1,3,2,0:T(8,128)S(1)}, bf16[16,256,128]{2,1,0:T(8,128)(2,1)}, bf16[16,128,2,32]{1,3,2,0:T(8,128)(2,1)S(1)}, bf16[2...) while((s32[]{:T(128)}, f32[16,128,2,32]{1,3,2,0:T(8,128)S(1)}, ...), condition=%wide.region_9.10_spmd.clone, body=%wide.region_6.9_spmd.clone.sunk | while | flops 13510144 | bytes 1613165 | solution.py:46
  112.6 0.9 constant_dynamic-slice_fusion.4
  114.7 0.9 constant_dynamic-slice_fusion.4
  116.8 0.9 constant_dynamic-slice_fusion.4
  118.8 0.9 constant_dynamic-slice_fusion.4
  120.9 0.9 constant_dynamic-slice_fusion.4
  122.9 0.9 constant_dynamic-slice_fusion.4
  125.0 0.9 constant_dynamic-slice_fusion.4
  127.0 0.9 constant_dynamic-slice_fusion.4
  129.1 0.9 constant_dynamic-slice_fusion.4
  131.2 0.9 constant_dynamic-slice_fusion.4
  133.2 0.9 constant_dynamic-slice_fusion.4
  135.3 0.9 constant_dynamic-slice_fusion.4
  137.3 0.9 constant_dynamic-slice_fusion.4
  139.4 0.9 constant_dynamic-slice_fusion.4
  141.5 0.9 constant_dynamic-slice_fusion.4
  143.5 0.9 constant_dynamic-slice_fusion.4
  145.7 32.9 %while.23 = (s32[]{:T(128)}, f32[16,128,2,32]{1,3,2,0:T(8,128)S(1)}, bf16[16,256,128]{2,1,0:T(8,128)(2,1)}, bf16[16,128,2,32]{1,3,2,0:T(8,128)(2,1)S(1)}, bf16[2...) while((s32[]{:T(128)}, f32[16,128,2,32]{1,3,2,0:T(8,128)S(1)}, ...), condition=%wide.region_13.14_spmd.clone, body=%wide.region_10.13_spmd.clone.sunk | while | flops 13510144 | bytes 1613165 | solution.py:46
  147.7 0.9 constant_dynamic-slice_fusion.5
  149.8 0.9 constant_dynamic-slice_fusion.5
  180.1 1.0 copy.50
  (334 shorter events, 61.2 us)
Async XLA Ops:
  6.5 70.5 %copy-start = (bf16[128,128]{1,0:T(8,128)(2,1)S(1)}, bf16[128,128]{1,0:T(8,128)(2,1)}, u32[]{:S(2)}) copy-start(bf16[128,128]{1,0:T(8,128)(2,1)} %param.19) | copy-start | bytes 98308
  6.5 45.9 %all-gather.4.cloned.1.call-start = ((), (), s32[]{:S(2)}) async-start(), calls=%async_computation.2 | async-start | bytes 1114112 | tf_op jit(solution)/shard_map/all_gather | solution.py:73
  6.5 0.7 copy-start.4
  9.1 0.7 copy-start.5
  9.8 0.9 copy-start.3
  52.5 21.7 %all-to-all-start = ((bf16[256,16,128]{2,1,0:T(8,128)(2,1)}), bf16[256,16,128]{2,1,0:T(8,128)(2,1)S(1)}, u32[]{:S(2)}, u32[]{:S(2)}) async-start(bf16[256,16,128]{2,1,0:T(8,128)(2,1)} %all-gather.4.cloned.1.call-done), calls=%async_computation | async-start | bytes 2097152 | tf_op jit(solution)/shard_map/all_to_all | solution.py:74
  56.1 56.5 %all-gather.6.cloned.1.call-start = ((), (), s32[]{:S(2)}) async-start(), calls=%async_computation.3 | async-start | bytes 1572864 | tf_op jit(solution)/shard_map/all_gather | solution.py:110
  71.7 0.9 copy-start.2
  76.2 0.7 copy-start.6
  76.3 1.2 copy-start.1
  78.2 0.7 copy-start.7
  80.1 0.7 copy-start.9
  102.5 9.4 %all-to-all-start.1 = ((bf16[4,256,128]{2,0,1:T(4,128)(2,1)}), bf16[4,256,128]{2,0,1:T(4,128)(2,1)S(1)}, u32[]{:S(2)}, u32[]{:S(2)}) async-start(bf16[4,256,128]{2,0,1:T(4,128)(2,1)} %all_gather.18), calls=%async_computation.1 | async-start | bytes 524288 | tf_op jit(solution)/shard_map/all_to_all | solution.py:94
  105.9 39.7 %all-gather.8.cloned.1.call-start = ((), (), s32[]{:S(2)}) async-start(), calls=%async_computation.4 | async-start | bytes 1572864 | tf_op jit(solution)/shard_map/all_gather | solution.py:110
  178.6 0.8 copy-start.8
Sparse Core Ops, SparseCore 0:
  11.9 40.5 all-gather.3
  80.2 19.3 all-gather.5
  108.3 19.0 all-gather.7
where the time goes:
time: 190 us; the launch traced here: 188 us
  waiting for transfers between devices  45 us (24%)
  local copies, waits for them, and re-layouts  44.5 us (23%)
  blocking collectives  37.1 us (20%)
  matrix products  35.2 us (19%)
  between operations  13.4 us (7%)
  starting transfers between devices  7.1 us (4%)
  other arithmetic  4.52 us (2%)
    all_gather x1, waiting for transfers between devices, body(): right_all = lax.all_gather(right_edge, 'row', axis=0, tiled=True)  40.7 us
    dynamic_slice x64, local copies, waits for them, and re-layouts, attend_heads(): return lax.map(attend_row, (query_pair, kv_all))  30.8 us
    all_gather x1, blocking collectives, body(): bias_rows = lax.all_gather(pair_bias, 'row', axis=1, tiled=True)  21.5 us
    all_gather x1, blocking collectives, body(): left_all = lax.all_gather(left_edge, 'col', axis=1, tiled=True)  15.6 us
    sub x32, matrix products, attend_row(): weights = jnp.exp(scores - row_top).astype(jnp.bfloat16)  13.7 us
    dot_general x32, matrix products, attend_row(): jnp.einsum('hjk,khd->jhd', weights, values_row, preferred_element_type=jn...  7.63 us
    dot_general x32, matrix products, attend_row(): jnp.einsum('jhd,khd->hjk', query_row, keys_row, preferred_element_type=jn...  7.44 us
    unnamed x21, local copies, waits for them, and re-layouts  6.7 us
  transfers between devices with their start and end apart: 5, of which 2 were waited for; matrix products, arithmetic and copies ran while one was open for 20% of the time, Pallas kernels for 0%

commit v1 on v0

--- a/solution.py
+++ b/solution.py
@@ -11,6 +11,27 @@
 SLOT = 64
 EPSILON = 1e-05
 NEG_SCORE = -1e30
+
+
+def ring_gather(x, axis, dim):
+    peers, index, span = (lax.axis_size(axis), lax.axis_index(axis), x.shape[dim])
+    right = [(i, (i + 1) % peers) for i in range(peers)]
+    left = [(i, (i - 1) % peers) for i in range(peers)]
+    out = jnp.zeros((*x.shape[:dim], peers * span, *x.shape[dim + 1 :]), x.dtype)
+    out = lax.dynamic_update_slice_in_dim(out, x, index * span, axis=dim)
+    from_left = from_right = x
+    half = peers // 2
+    for hop in range(1, half + 1):
+        from_left = lax.ppermute(from_left, axis, right)
+        out = lax.dynamic_update_slice_in_dim(
+            out, from_left, (index - hop) % peers * span, axis=dim
+        )
+        if hop < peers - half:
+            from_right = lax.ppermute(from_right, axis, left)
+            out = lax.dynamic_update_slice_in_dim(
+                out, from_right, (index + hop) % peers * span, axis=dim
+            )
+    return out
 
 
 def layer_norm(values, norm_gain):
@@ -70,7 +91,7 @@
         * group_proj[..., 3 * CH : 4 * CH]
         * pair_live
     ).astype(jnp.bfloat16)
-    right_all = lax.all_gather(right_edge, "row", axis=0, tiled=True)
+    right_all = ring_gather(right_edge, "row", 0)
     right_cols = lax.all_to_all(right_all, "col", split_axis=0, concat_axis=1, tiled=True)
     left_all = lax.all_gather(left_edge, "col", axis=1, tiled=True)
     tri_sum = jnp.einsum("ikc,jkc->jic", left_all, right_cols, preferred_element_type=jnp.float32)

time: 190 us -> 196 us (1.032)
  starting transfers between devices: 7.1 us -> 39.7 us
  waiting for transfers between devices: 45 us -> 14.9 us
  local copies, waits for them, and re-layouts: 44.5 us -> 55 us
  blocking collectives: 37.1 us -> 29.7 us
    all_gather x1 -> x0, waiting for transfers between devices: 40.7 us -> none  [body(): right_all = lax.all_gather(right_edge, 'row', axis=0, tiled=True)]
    ppermute x0 -> x15, starting transfers between devices: none -> 32.6 us  [the longest x7 32.1 us: ring_gather(): from_right = lax.ppermute(from_right, axis, left)]
    ppermute x0 -> x15, waiting for transfers between devices: none -> 10.6 us  [the longest x8 10.4 us: ring_gather(): from_left = lax.ppermute(from_left, axis, right)]
    dynamic_update_slice x0 -> x15, local copies, waits for them, and re-layouts: none -> 9.34 us  [the longest x8 4.98 us: ring_gather(): lax.dynamic_update_slice_in_dim(out, from_left, (index - hop) % peers * s...]
    all_gather x1, blocking collectives: 15.6 us -> 10.4 us  [body(): left_all = lax.all_gather(left_edge, 'col', axis=1, tiled=True)]
    all_gather x1, blocking collectives: 21.5 us -> 19.2 us  [body(): bias_rows = lax.all_gather(pair_bias, 'row', axis=1, tiled=True)]
  transfers between devices with their start and end apart: 5 -> 19, of which waited for: 2 -> 11; matrix products, arithmetic and copies ran while one was open for 20% -> 24% of each run, Pallas kernels for 0% -> 0%
where the time goes in v1:
time: 196 us; the launch traced here: 194 us
  local copies, waits for them, and re-layouts  55 us (28%)
  starting transfers between devices  39.7 us (20%)
  matrix products  35.1 us (18%)
  blocking collectives  29.7 us (15%)
  waiting for transfers between devices  14.9 us (8%)
  between operations  14 us (7%)
  other arithmetic  4.61 us (2%)
    ppermute x7, starting transfers between devices, ring_gather(): from_right = lax.ppermute(from_right, axis, left)  32.1 us
    dynamic_slice x64, local copies, waits for them, and re-layouts, attend_heads(): return lax.map(attend_row, (query_pair, kv_all))  30.8 us
    all_gather x1, blocking collectives, body(): bias_rows = lax.all_gather(pair_bias, 'row', axis=1, tiled=True)  19.2 us
    sub x32, matrix products, attend_row(): weights = jnp.exp(scores - row_top).astype(jnp.bfloat16)  13.7 us
    all_gather x1, blocking collectives, body(): left_all = lax.all_gather(left_edge, 'col', axis=1, tiled=True)  10.4 us
    ppermute x8, waiting for transfers between devices, ring_gather(): from_left = lax.ppermute(from_left, axis, right)  10.4 us
    dot_general x32, matrix products, attend_row(): jnp.einsum('hjk,khd->jhd', weights, values_row, preferred_element_type=jn...  7.63 us
    dot_general x32, matrix products, attend_row(): jnp.einsum('jhd,khd->hjk', query_row, keys_row, preferred_element_type=jn...  7.44 us
  transfers between devices with their start and end apart: 19, of which 11 were waited for; matrix products, arithmetic and copies ran while one was open for 24% of the time, Pallas kernels for 0%

profile of v1, /device:TPU:0, one launch (start us, length us, event | category | flops | bytes accessed | tf_op | source)
XLA Modules:
  0.0 193.9 jit_solution(4423174295901621711)
XLA Ops:
  7.5 1.3 copy.50
  11.0 1.2 broadcast_in_dim.48
  13.4 4.9 %collective-permute-start.1 = (bf16[16,16,128]{2,1,0:T(8,128)(2,1)S(1)}, bf16[16,16,128]{2,1,0:T(8,128)(2,1)S(1)}, u32[]{:S(2)}, u32[]{:S(2)}) collective-permute-start(bf16[16,16,128]{2,1,0:T(8,128)(2,1)S(1)} %get-tuple-element.162), channel_id=1, source_target_pairs={{0,30},{2,0},{4,2},{6,4},{8,6},{10,8},{12,10},{14,12},{16,14},{18,... | collective-permute-start | bytes 196616 | tf_op jit(solution)/shard_map/ppermute | solution.py:30
  18.7 1.7 collective-permute-done
  20.4 4.4 %collective-permute-start.3 = (bf16[16,16,128]{2,1,0:T(8,128)(2,1)S(1)}, bf16[16,16,128]{2,1,0:T(8,128)(2,1)S(1)}, u32[]{:S(2)}, u32[]{:S(2)}) collective-permute-start(bf16[16,16,128]{2,1,0:T(8,128)(2,1)S(1)} %collective-permute-done.1), channel_id=1, source_target_pairs={{0,30},{2,0},{4,2},{6,4},{8,6},{10,8},{12,10},{14,12},{16,14},{18,... | collective-permute-start | bytes 196616 | tf_op jit(solution)/shard_map/ppermute | solution.py:30
  26.8 4.4 %collective-permute-start.5 = (bf16[16,16,128]{2,1,0:T(8,128)(2,1)S(1)}, bf16[16,16,128]{2,1,0:T(8,128)(2,1)S(1)}, u32[]{:S(2)}, u32[]{:S(2)}) collective-permute-start(bf16[16,16,128]{2,1,0:T(8,128)(2,1)S(1)} %collective-permute-done.3), channel_id=1, source_target_pairs={{0,30},{2,0},{4,2},{6,4},{8,6},{10,8},{12,10},{14,12},{16,14},{18,... | collective-permute-start | bytes 196616 | tf_op jit(solution)/shard_map/ppermute | solution.py:30
  33.2 4.5 %collective-permute-start.7 = (bf16[16,16,128]{2,1,0:T(8,128)(2,1)S(1)}, bf16[16,16,128]{2,1,0:T(8,128)(2,1)S(1)}, u32[]{:S(2)}, u32[]{:S(2)}) collective-permute-start(bf16[16,16,128]{2,1,0:T(8,128)(2,1)S(1)} %collective-permute-done.5), channel_id=1, source_target_pairs={{0,30},{2,0},{4,2},{6,4},{8,6},{10,8},{12,10},{14,12},{16,14},{18,... | collective-permute-start | bytes 196616 | tf_op jit(solution)/shard_map/ppermute | solution.py:30
  39.6 4.6 %collective-permute-start.9 = (bf16[16,16,128]{2,1,0:T(8,128)(2,1)S(1)}, bf16[16,16,128]{2,1,0:T(8,128)(2,1)S(1)}, u32[]{:S(2)}, u32[]{:S(2)}) collective-permute-start(bf16[16,16,128]{2,1,0:T(8,128)(2,1)S(1)} %collective-permute-done.7), channel_id=1, source_target_pairs={{0,30},{2,0},{4,2},{6,4},{8,6},{10,8},{12,10},{14,12},{16,14},{18,... | collective-permute-start | bytes 196616 | tf_op jit(solution)/shard_map/ppermute | solution.py:30
  46.1 4.6 %collective-permute-start.11 = (bf16[16,16,128]{2,1,0:T(8,128)(2,1)S(1)}, bf16[16,16,128]{2,1,0:T(8,128)(2,1)S(1)}, u32[]{:S(2)}, u32[]{:S(2)}) collective-permute-start(bf16[16,16,128]{2,1,0:T(8,128)(2,1)S(1)} %collective-permute-done.9), channel_id=1, source_target_pairs={{0,30},{2,0},{4,2},{6,4},{8,6},{10,8},{12,10},{14,12},{16,14},{18,... | collective-permute-start | bytes 196616 | tf_op jit(solution)/shard_map/ppermute | solution.py:30
  52.6 4.6 %collective-permute-start.13 = (bf16[16,16,128]{2,1,0:T(8,128)(2,1)S(1)}, bf16[16,16,128]{2,1,0:T(8,128)(2,1)S(1)}, u32[]{:S(2)}, u32[]{:S(2)}) collective-permute-start(bf16[16,16,128]{2,1,0:T(8,128)(2,1)S(1)} %collective-permute-done.11), channel_id=1, source_target_pairs={{0,30},{2,0},{4,2},{6,4},{8,6},{10,8},{12,10},{14,12},{16,14},{18,... | collective-permute-start | bytes 196616 | tf_op jit(solution)/shard_map/ppermute | solution.py:30
  60.1 5.1 %collective-permute-done.14 = bf16[16,16,128]{2,1,0:T(8,128)(2,1)S(1)} collective-permute-done((bf16[16,16,128]{2,1,0:T(8,128)(2,1)S(1)}, bf16[16,16,128]{2,1,0:T(8,128)(2,1)S(1)}, u32[]{:S(2)}, u32[]{:S(2)}) %collective-permute-start.14) | collective-permute-done | bytes 65568 | tf_op jit(solution)/shard_map/ppermute | solution.py:25
  65.9 3.6 %all-to-all-start = ((bf16[256,16,128]{2,1,0:T(8,128)(2,1)}), bf16[256,16,128]{2,1,0:T(8,128)(2,1)S(1)}, u32[]{:S(2)}, u32[]{:S(2)}) async-start(bf16[256,16,128]{2,1,0:T(8,128)(2,1)} %constant_dynamic-update-slice_fusion), calls=%async_computation | async-start | bytes 2097152 | tf_op jit(solution)/shard_map/all_to_all | solution.py:95
  69.5 10.4 %all_gather.12 = bf16[16,32,128]{2,1,0:T(8,128)(2,1)S(1)} all-gather(bf16[16,16,128]{2,1,0:T(8,128)(2,1)S(1)} %fusion.70), channel_id=1, replica_groups=mesh['row'=16,'col'=2] {'col'}, dimensions={1}, use_global_device_ids=true | all-gather | bytes 196608 | tf_op jit(solution)/shard_map/all_gather | solution.py:96
  80.9 1.4 fusion.45
  82.4 1.5 copy.54
  87.0 1.2 convolution_convert_fusion.2
  89.2 19.2 %all_gather.14 = bf16[4,256,128]{2,0,1:T(4,128)(2,1)} all-gather(bf16[4,16,128]{2,0,1:T(4,128)(2,1)S(1)} %fusion.53), channel_id=1, replica_groups=mesh['row'=16,'col'=2] {'row'}, dimensions={1}, use_global_device_ids=true | all-gather | bytes 278528 | tf_op jit(solution)/shard_map/all_gather | solution.py:114
  108.4 3.4 %all-to-all-start.1 = ((bf16[4,256,128]{2,0,1:T(4,128)(2,1)}), bf16[4,256,128]{2,0,1:T(4,128)(2,1)S(1)}, u32[]{:S(2)}, u32[]{:S(2)}) async-start(bf16[4,256,128]{2,0,1:T(4,128)(2,1)} %all_gather.14), calls=%async_computation.1 | async-start | bytes 524288 | tf_op jit(solution)/shard_map/all_to_all | solution.py:115
  111.9 1.2 convolution_convert_fusion.1
  113.5 4.2 %all-to-all-done.1 = bf16[4,256,128]{2,0,1:T(4,128)(2,1)S(1)} async-done(((bf16[4,256,128]{2,0,1:T(4,128)(2,1)}), bf16[4,256,128]{2,0,1:T(4,128)(2,1)S(1)}, u32[]{:S(2)}, u32[]{:S(2)}) %all-to-all-start.1) | async-done | bytes 262176 | tf_op jit(solution)/shard_map/all_to_all | solution.py:115
  118.5 33.0 %while.22 = (s32[]{:T(128)}, f32[16,128,2,32]{1,3,2,0:T(8,128)S(1)}, bf16[16,256,128]{2,1,0:T(8,128)(2,1)}, bf16[16,128,2,32]{1,3,2,0:T(8,128)(2,1)S(1)}, bf16[2...) while((s32[]{:T(128)}, f32[16,128,2,32]{1,3,2,0:T(8,128)S(1)}, ...), condition=%wide.region_9.10_spmd.clone, body=%wide.region_6.9_spmd.clone.sunk | while | flops 13510144 | bytes 1613165 | solution.py:67
  120.6 0.9 constant_dynamic-slice_fusion.4
  122.7 0.9 constant_dynamic-slice_fusion.4
  124.7 0.9 constant_dynamic-slice_fusion.4
  126.8 0.9 constant_dynamic-slice_fusion.4
  128.9 0.9 constant_dynamic-slice_fusion.4
  130.9 0.9 constant_dynamic-slice_fusion.4
  133.0 0.9 constant_dynamic-slice_fusion.4
  135.0 0.9 constant_dynamic-slice_fusion.4
  137.1 0.9 constant_dynamic-slice_fusion.4
  151.6 32.9 %while.23 = (s32[]{:T(128)}, f32[16,128,2,32]{1,3,2,0:T(8,128)S(1)}, bf16[16,256,128]{2,1,0:T(8,128)(2,1)}, bf16[16,128,2,32]{1,3,2,0:T(8,128)(2,1)S(1)}, bf16[2...) while((s32[]{:T(128)}, f32[16,128,2,32]{1,3,2,0:T(8,128)S(1)}, ...), condition=%wide.region_13.14_spmd.clone, body=%wide.region_10.13_spmd.clone.sunk | while | flops 13510144 | bytes 1613165 | solution.py:67
  186.0 1.0 copy.71
  (378 shorter events, 82.7 us)
Async XLA Ops:
  6.5 78.7 %copy-start = (bf16[128,128]{1,0:T(8,128)(2,1)S(1)}, bf16[128,128]{1,0:T(8,128)(2,1)}, u32[]{:S(2)}) copy-start(bf16[128,128]{1,0:T(8,128)(2,1)} %param.19) | copy-start | bytes 98308
  6.5 0.7 copy-start.4
  9.1 0.7 copy-start.5
  9.8 0.9 copy-start.3
  12.9 7.5 %collective-permute-start = (bf16[16,16,128]{2,1,0:T(8,128)(2,1)S(1)}, bf16[16,16,128]{2,1,0:T(8,128)(2,1)S(1)}, u32[]{:S(2)}, u32[]{:S(2)}) collective-permute-start(bf16[16,16,128]{2,1,0:T(8,128)(2,1)S(1)} %get-tuple-element.162), channel_id=1, source_target_pairs={{0,2},{2,4},{4,6},{6,8},{8,10},{10,12},{12,14},{14,16},{16,18},{18... | collective-permute-start | bytes 196616 | tf_op jit(solution)/shard_map/ppermute | solution.py:25
  13.4 7.0 %collective-permute-start.1 = (bf16[16,16,128]{2,1,0:T(8,128)(2,1)S(1)}, bf16[16,16,128]{2,1,0:T(8,128)(2,1)S(1)}, u32[]{:S(2)}, u32[]{:S(2)}) collective-permute-start(bf16[16,16,128]{2,1,0:T(8,128)(2,1)S(1)} %get-tuple-element.162), channel_id=1, source_target_pairs={{0,30},{2,0},{4,2},{6,4},{8,6},{10,8},{12,10},{14,12},{16,14},{18,... | collective-permute-start | bytes 196616 | tf_op jit(solution)/shard_map/ppermute | solution.py:30
  20.4 6.4 %collective-permute-start.2 = (bf16[16,16,128]{2,1,0:T(8,128)(2,1)S(1)}, bf16[16,16,128]{2,1,0:T(8,128)(2,1)S(1)}, u32[]{:S(2)}, u32[]{:S(2)}) collective-permute-start(bf16[16,16,128]{2,1,0:T(8,128)(2,1)S(1)} %collective-permute-done), channel_id=1, source_target_pairs={{0,2},{2,4},{4,6},{6,8},{8,10},{10,12},{12,14},{14,16},{16,18},{18... | collective-permute-start | bytes 196616 | tf_op jit(solution)/shard_map/ppermute | solution.py:25
  20.4 6.4 %collective-permute-start.3 = (bf16[16,16,128]{2,1,0:T(8,128)(2,1)S(1)}, bf16[16,16,128]{2,1,0:T(8,128)(2,1)S(1)}, u32[]{:S(2)}, u32[]{:S(2)}) collective-permute-start(bf16[16,16,128]{2,1,0:T(8,128)(2,1)S(1)} %collective-permute-done.1), channel_id=1, source_target_pairs={{0,30},{2,0},{4,2},{6,4},{8,6},{10,8},{12,10},{14,12},{16,14},{18,... | collective-permute-start | bytes 196616 | tf_op jit(solution)/shard_map/ppermute | solution.py:30
  26.8 6.4 %collective-permute-start.4 = (bf16[16,16,128]{2,1,0:T(8,128)(2,1)S(1)}, bf16[16,16,128]{2,1,0:T(8,128)(2,1)S(1)}, u32[]{:S(2)}, u32[]{:S(2)}) collective-permute-start(bf16[16,16,128]{2,1,0:T(8,128)(2,1)S(1)} %collective-permute-done.2), channel_id=1, source_target_pairs={{0,2},{2,4},{4,6},{6,8},{8,10},{10,12},{12,14},{14,16},{16,18},{18... | collective-permute-start | bytes 196616 | tf_op jit(solution)/shard_map/ppermute | solution.py:25
  26.8 6.4 %collective-permute-start.5 = (bf16[16,16,128]{2,1,0:T(8,128)(2,1)S(1)}, bf16[16,16,128]{2,1,0:T(8,128)(2,1)S(1)}, u32[]{:S(2)}, u32[]{:S(2)}) collective-permute-start(bf16[16,16,128]{2,1,0:T(8,128)(2,1)S(1)} %collective-permute-done.3), channel_id=1, source_target_pairs={{0,30},{2,0},{4,2},{6,4},{8,6},{10,8},{12,10},{14,12},{16,14},{18,... | collective-permute-start | bytes 196616 | tf_op jit(solution)/shard_map/ppermute | solution.py:30
  33.2 6.4 %collective-permute-start.6 = (bf16[16,16,128]{2,1,0:T(8,128)(2,1)S(1)}, bf16[16,16,128]{2,1,0:T(8,128)(2,1)S(1)}, u32[]{:S(2)}, u32[]{:S(2)}) collective-permute-start(bf16[16,16,128]{2,1,0:T(8,128)(2,1)S(1)} %collective-permute-done.4), channel_id=1, source_target_pairs={{0,2},{2,4},{4,6},{6,8},{8,10},{10,12},{12,14},{14,16},{16,18},{18... | collective-permute-start | bytes 196616 | tf_op jit(solution)/shard_map/ppermute | solution.py:25
  33.2 6.4 %collective-permute-start.7 = (bf16[16,16,128]{2,1,0:T(8,128)(2,1)S(1)}, bf16[16,16,128]{2,1,0:T(8,128)(2,1)S(1)}, u32[]{:S(2)}, u32[]{:S(2)}) collective-permute-start(bf16[16,16,128]{2,1,0:T(8,128)(2,1)S(1)} %collective-permute-done.5), channel_id=1, source_target_pairs={{0,30},{2,0},{4,2},{6,4},{8,6},{10,8},{12,10},{14,12},{16,14},{18,... | collective-permute-start | bytes 196616 | tf_op jit(solution)/shard_map/ppermute | solution.py:30
  39.6 6.4 %collective-permute-start.8 = (bf16[16,16,128]{2,1,0:T(8,128)(2,1)S(1)}, bf16[16,16,128]{2,1,0:T(8,128)(2,1)S(1)}, u32[]{:S(2)}, u32[]{:S(2)}) collective-permute-start(bf16[16,16,128]{2,1,0:T(8,128)(2,1)S(1)} %collective-permute-done.6), channel_id=1, source_target_pairs={{0,2},{2,4},{4,6},{6,8},{8,10},{10,12},{12,14},{14,16},{16,18},{18... | collective-permute-start | bytes 196616 | tf_op jit(solution)/shard_map/ppermute | solution.py:25
  39.6 6.5 %collective-permute-start.9 = (bf16[16,16,128]{2,1,0:T(8,128)(2,1)S(1)}, bf16[16,16,128]{2,1,0:T(8,128)(2,1)S(1)}, u32[]{:S(2)}, u32[]{:S(2)}) collective-permute-start(bf16[16,16,128]{2,1,0:T(8,128)(2,1)S(1)} %collective-permute-done.7), channel_id=1, source_target_pairs={{0,30},{2,0},{4,2},{6,4},{8,6},{10,8},{12,10},{14,12},{16,14},{18,... | collective-permute-start | bytes 196616 | tf_op jit(solution)/shard_map/ppermute | solution.py:30
  46.0 6.5 %collective-permute-start.10 = (bf16[16,16,128]{2,1,0:T(8,128)(2,1)S(1)}, bf16[16,16,128]{2,1,0:T(8,128)(2,1)S(1)}, u32[]{:S(2)}, u32[]{:S(2)}) collective-permute-start(bf16[16,16,128]{2,1,0:T(8,128)(2,1)S(1)} %collective-permute-done.8), channel_id=1, source_target_pairs={{0,2},{2,4},{4,6},{6,8},{8,10},{10,12},{12,14},{14,16},{16,18},{18... | collective-permute-start | bytes 196616 | tf_op jit(solution)/shard_map/ppermute | solution.py:25
  46.1 6.5 %collective-permute-start.11 = (bf16[16,16,128]{2,1,0:T(8,128)(2,1)S(1)}, bf16[16,16,128]{2,1,0:T(8,128)(2,1)S(1)}, u32[]{:S(2)}, u32[]{:S(2)}) collective-permute-start(bf16[16,16,128]{2,1,0:T(8,128)(2,1)S(1)} %collective-permute-done.9), channel_id=1, source_target_pairs={{0,30},{2,0},{4,2},{6,4},{8,6},{10,8},{12,10},{14,12},{16,14},{18,... | collective-permute-start | bytes 196616 | tf_op jit(solution)/shard_map/ppermute | solution.py:30
  52.5 6.4 %collective-permute-start.12 = (bf16[16,16,128]{2,1,0:T(8,128)(2,1)S(1)}, bf16[16,16,128]{2,1,0:T(8,128)(2,1)S(1)}, u32[]{:S(2)}, u32[]{:S(2)}) collective-permute-start(bf16[16,16,128]{2,1,0:T(8,128)(2,1)S(1)} %collective-permute-done.10), channel_id=1, source_target_pairs={{0,2},{2,4},{4,6},{6,8},{8,10},{10,12},{12,14},{14,16},{16,18},{18... | collective-permute-start | bytes 196616 | tf_op jit(solution)/shard_map/ppermute | solution.py:25
  52.6 6.9 %collective-permute-start.13 = (bf16[16,16,128]{2,1,0:T(8,128)(2,1)S(1)}, bf16[16,16,128]{2,1,0:T(8,128)(2,1)S(1)}, u32[]{:S(2)}, u32[]{:S(2)}) collective-permute-start(bf16[16,16,128]{2,1,0:T(8,128)(2,1)S(1)} %collective-permute-done.11), channel_id=1, source_target_pairs={{0,30},{2,0},{4,2},{6,4},{8,6},{10,8},{12,10},{14,12},{16,14},{18,... | collective-permute-start | bytes 196616 | tf_op jit(solution)/shard_map/ppermute | solution.py:30
  58.9 6.4 %collective-permute-start.14 = (bf16[16,16,128]{2,1,0:T(8,128)(2,1)S(1)}, bf16[16,16,128]{2,1,0:T(8,128)(2,1)S(1)}, u32[]{:S(2)}, u32[]{:S(2)}) collective-permute-start(bf16[16,16,128]{2,1,0:T(8,128)(2,1)S(1)} %collective-permute-done.12), channel_id=1, source_target_pairs={{0,2},{2,4},{4,6},{6,8},{8,10},{10,12},{12,14},{14,16},{16,18},{18... | collective-permute-start | bytes 196616 | tf_op jit(solution)/shard_map/ppermute | solution.py:25
  65.9 16.5 %all-to-all-start = ((bf16[256,16,128]{2,1,0:T(8,128)(2,1)}), bf16[256,16,128]{2,1,0:T(8,128)(2,1)S(1)}, u32[]{:S(2)}, u32[]{:S(2)}) async-start(bf16[256,16,128]{2,1,0:T(8,128)(2,1)} %constant_dynamic-update-slice_fusion), calls=%async_computation | async-start | bytes 2097152 | tf_op jit(solution)/shard_map/all_to_all | solution.py:95
  69.5 49.0 %all-gather.3.cloned.1.call-start = ((), (), s32[]{:S(2)}) async-start(), calls=%async_computation.2 | async-start | bytes 1572864 | tf_op jit(solution)/shard_map/all_gather | solution.py:131
  79.9 0.9 copy-start.2
  84.3 0.7 copy-start.6
  84.5 1.2 copy-start.1
  86.3 0.7 copy-start.7
  88.2 0.7 copy-start.9
  108.4 9.4 %all-to-all-start.1 = ((bf16[4,256,128]{2,0,1:T(4,128)(2,1)}), bf16[4,256,128]{2,0,1:T(4,128)(2,1)S(1)}, u32[]{:S(2)}, u32[]{:S(2)}) async-start(bf16[4,256,128]{2,0,1:T(4,128)(2,1)} %all_gather.14), calls=%async_computation.1 | async-start | bytes 524288 | tf_op jit(solution)/shard_map/all_to_all | solution.py:115
  111.9 39.7 %all-gather.5.cloned.1.call-start = ((), (), s32[]{:S(2)}) async-start(), calls=%async_computation.3 | async-start | bytes 1572864 | tf_op jit(solution)/shard_map/all_gather | solution.py:131
  184.5 0.8 copy-start.8
Sparse Core Ops, SparseCore 0:
  88.3 17.2 all-gather.2
  114.2 20.4 all-gather.4
